TPU v7x, 32 devices: a whole 2x2x4 slice. The times are simulated.
32 devices in a mesh: dp: 8 (over z, x), mlp: 4 (over y, core).
Axes of the slice: x: 2, y: 2, z: 4, core: 2. Of those that a mesh axis runs over, the one named last changes fastest.
Arguments:
- tokens: bfloat16 [32768, 768], P(('dp', 'mlp')), may hold values from -6 to 6
- cotangent: bfloat16 [32768, 768], P(('dp', 'mlp')), may hold values from -6 to 6
- vectors: float32 [14, 768], replicated
- vector_moments: float32 [14, 768], replicated, may hold values from 819.2 to 26214.4
- decays: float32 [2], replicated, may hold values from 0.9 to 0.98
- owner: int32 [4, 3], replicated, may hold values from 0 to 7, as said below
- master_slots: float32 [8, 4, 768, 768], P('dp', 'mlp'), as said below
- left_slots: float32 [8, 4, 768, 768], P('dp', 'mlp'), as said below
- right_slots: float32 [8, 4, 768, 768], P('dp', 'mlp'), as said below
- left_roots: float32 [8, 4, 768, 768], P('dp', 'mlp'), as said below
- right_roots: float32 [8, 4, 768, 768], P('dp', 'mlp'), as said below
- grid_height: int32 [128], P(('dp', 'mlp')), may hold values from 8 to 24, as said below
- grid_width: int32 [128], P(('dp', 'mlp')), may hold values from 8 to 24, as said below
- patch_rows: int32 [32768], P(('dp', 'mlp')), may hold values from 0 to 23, as said below
- patch_cols: int32 [32768], P(('dp', 'mlp')), may hold values from 0 to 23, as said below
- segment: int32 [32768], P(('dp', 'mlp')), may hold values from 0 to 3, as said below
Outputs:
- output: bfloat16 [32768, 768], P(('dp', 'mlp'))
- input_grad: float32 [32768, 768], P(('dp', 'mlp'))
- slot_grads: float32 [8, 4, 768, 768], P('dp', 'mlp')
- new_left: float32 [8, 4, 768, 768], P('dp', 'mlp')
- new_right: float32 [8, 4, 768, 768], P('dp', 'mlp')
- new_master: float32 [8, 4, 768, 768], P('dp', 'mlp')
- vector_grads: float32 [14, 768], P(None, 'mlp')
- new_vector_moments: float32 [14, 768], P(None, 'mlp')
- new_vectors: float32 [14, 768], P(None, 'mlp')
Inputs may be any that keep to these rules, and one draw needn't show every extreme that they name: `owner`: the entries of a row differ; block kind 0 of row m is the m-th of the query, key, value and output projections, kind 1 the m-th 768 columns of the up projection, kind 2 the m-th 768 rows of the down projection. `master_slots`: slot (owner[m,k], m) holds block kind k of row m; the other slots are unused. `left_slots`: symmetric and positive definite. `right_slots`: symmetric and positive definite. `left_roots`: symmetric and positive definite. `right_roots`: symmetric and positive definite. `grid_height`: each image is 16 patches along one side; the other sides of one device's images add up to 64. `grid_width`: as grid_height. `patch_rows`: each device's patches hold its images whole, one after another in the order of their numbers, each in raster order. `patch_cols`: as patch_rows. `segment`: never falls within a device's patches.
All inputs are finite; a program needn't handle non-finite values.
Results may differ from a plain program's by a relative error of at most 0.014.
Values may be sent and summed in bfloat16 or wider, within the bound.
A program may use at most 192 MiB of HBM per device.

v0:
```python
import math
import jax
import jax.numpy as jnp
from jax import lax
from jax.sharding import PartitionSpec as P

HEADS = 12
GRID_BASE = 16
NORM_EPSILON = 1e-06
GRAFT_EPSILON = 1e-06
STEP_EPSILON = 1e-08
RATE_MATRIX = 0.04
RATE_VECTOR = 0.02
MASKED_SCORE = -1e30


def layer_norm(values, gain_row, shift_row):
    centred = values - jnp.mean(values, axis=-1, keepdims=True)
    spread = jnp.mean(centred * centred, axis=-1, keepdims=True)
    return centred * lax.rsqrt(spread + NORM_EPSILON) * gain_row + shift_row


def exact_gelu(values):
    return jax.nn.gelu(values, approximate=False)


def rotate_pairs(flat_values, freq_row, rows_pos, cols_pos):
    tokens_here = flat_values.shape[0]
    values = flat_values.reshape(tokens_here, HEADS, -1)
    half_size = values.shape[-1] // 2
    middle = freq_row.shape[0] // 2
    freq_cols = freq_row[:middle].reshape(HEADS, half_size)
    freq_rows = freq_row[middle:].reshape(HEADS, half_size)
    angle_grid = (
        rows_pos[:, None, None] * freq_rows[None] + cols_pos[:, None, None] * freq_cols[None]
    )
    cosine = jnp.cos(angle_grid)
    sine_part = jnp.sin(angle_grid)
    first_half = values[..., :half_size]
    second = values[..., half_size:]
    turned = jnp.concatenate(
        [first_half * cosine - second * sine_part, second * cosine + first_half * sine_part],
        axis=-1,
    )
    return turned.reshape(tokens_here, -1)


def patch_positions(segment_ids, heights_in, widths_in, rows_in, cols_in):
    images_here = heights_in.shape[0]
    matches = segment_ids[:, None] == jnp.arange(images_here, dtype=jnp.int32)[None, :]
    heights = jnp.sum(jnp.where(matches, heights_in[None, :], 0), axis=1).astype(jnp.float32)
    widths = jnp.sum(jnp.where(matches, widths_in[None, :], 0), axis=1).astype(jnp.float32)
    rows_pos = rows_in.astype(jnp.float32) * GRID_BASE / heights
    cols_pos = cols_in.astype(jnp.float32) * GRID_BASE / widths
    return (rows_pos, cols_pos)


def heads_first(flat_values):
    return jnp.swapaxes(flat_values.reshape(flat_values.shape[0], HEADS, -1), 0, 1)


def tokens_first(stacked):
    return jnp.swapaxes(stacked, 0, 1).reshape(stacked.shape[1], -1)


def local(
    tokens,
    cotangent,
    vectors,
    vector_moments,
    decays,
    owner,
    master_slots,
    left_slots,
    right_slots,
    left_roots,
    right_roots,
    grid_height,
    grid_width,
    patch_rows,
    patch_cols,
    segment,
):
    dp_index = lax.axis_index("dp")
    mlp_index = lax.axis_index("mlp")
    groups_mlp = lax.axis_size("mlp")
    model_width = tokens.shape[1]
    rows_here = tokens.shape[0]
    owner_row = jnp.take(owner, mlp_index, axis=0)
    holds_block = owner_row == dp_index
    owned_blocks = jnp.where(holds_block[:, None, None], master_slots[0, 0][None], 0.0)
    blocks = lax.psum(owned_blocks, "dp")
    blocks_low = blocks.astype(jnp.bfloat16)
    up_rows = vectors[8 : 8 + groups_mlp]
    down_bias = vectors[8 + groups_mlp]
    freq_row = vectors[9 + groups_mlp]
    every_block = lax.all_gather(blocks_low[None], "mlp", axis=0, tiled=True)
    attention_weights = every_block[:, 0]
    up_weight = every_block[:, 1]
    down_weight = every_block[:, 2]
    up_bias = up_rows.reshape(-1)
    inputs = tokens.astype(jnp.float32)
    norm_one, norm_one_back = jax.vjp(layer_norm, inputs, vectors[0], vectors[1])
    norm_one_low = norm_one.astype(jnp.bfloat16)
    query_lin = (
        jnp.dot(norm_one_low, attention_weights[0], preferred_element_type=jnp.float32) + vectors[2]
    )
    key_lin = (
        jnp.dot(norm_one_low, attention_weights[1], preferred_element_type=jnp.float32) + vectors[3]
    )
    value_low = (
        jnp.dot(norm_one_low, attention_weights[2], preferred_element_type=jnp.float32) + vectors[4]
    ).astype(jnp.bfloat16)
    rows_pos, cols_pos = patch_positions(segment, grid_height, grid_width, patch_rows, patch_cols)

    def rotary_map(flat_values, freq_values):
        return rotate_pairs(flat_values, freq_values, rows_pos, cols_pos)

    query_rot, query_back = jax.vjp(rotary_map, query_lin, freq_row)
    key_rot, key_back = jax.vjp(rotary_map, key_lin, freq_row)
    query_heads = heads_first(query_rot.astype(jnp.bfloat16))
    key_heads = heads_first(key_rot.astype(jnp.bfloat16))
    value_heads = heads_first(value_low)
    same_image = segment[:, None] == segment[None, :]
    score_scale = 1.0 / math.sqrt(model_width // HEADS)

    def head_scores(query_head, key_head):
        scores = jnp.dot(query_head, key_head.T, preferred_element_type=jnp.float32) * score_scale
        return jnp.where(same_image, scores, MASKED_SCORE)

    def head_forward(pieces):
        query_head, key_head, value_head = pieces
        scores = head_scores(query_head, key_head)
        row_peak = jnp.max(scores, axis=1, keepdims=True)
        exponent = jnp.exp(scores - row_peak)
        row_total = jnp.sum(exponent, axis=1, keepdims=True)
        weights_low = (exponent / row_total).astype(jnp.bfloat16)
        attended = jnp.dot(weights_low, value_head, preferred_element_type=jnp.float32)
        return (attended, (row_peak + jnp.log(row_total))[:, 0])

    attended_heads, log_totals = lax.map(head_forward, (query_heads, key_heads, value_heads))
    attended_low = tokens_first(attended_heads).astype(jnp.bfloat16)
    branch_one = (
        jnp.dot(attended_low, attention_weights[3], preferred_element_type=jnp.float32) + vectors[5]
    )
    middle = inputs + branch_one
    norm_two, norm_two_back = jax.vjp(layer_norm, middle, vectors[6], vectors[7])
    norm_two_low = norm_two.astype(jnp.bfloat16)
    pre_act = (
        jnp.einsum(
            "td,mde->tme", norm_two_low, up_weight, preferred_element_type=jnp.float32
        ).reshape(rows_here, -1)
        + up_bias
    )
    activation, gelu_back = jax.vjp(exact_gelu, pre_act)
    activation_blocks = activation.astype(jnp.bfloat16).reshape(rows_here, groups_mlp, -1)
    branch_two = (
        jnp.einsum(
            "tme,med->td", activation_blocks, down_weight, preferred_element_type=jnp.float32
        )
        + down_bias
    )
    grad_act = jnp.einsum(
        "td,med->tme", cotangent, down_weight, preferred_element_type=jnp.float32
    ).reshape(rows_here, -1)
    grad_down = jnp.einsum(
        "tme,td->med", activation_blocks, cotangent, preferred_element_type=jnp.float32
    )
    grad_pre_blocks = gelu_back(grad_act)[0].astype(jnp.bfloat16).reshape(rows_here, groups_mlp, -1)
    grad_up = jnp.einsum(
        "td,tme->mde", norm_two_low, grad_pre_blocks, preferred_element_type=jnp.float32
    )
    up_grad_rows = jnp.sum(grad_pre_blocks, axis=0, dtype=jnp.float32)
    grad_norm_two = jnp.einsum(
        "tme,mde->td", grad_pre_blocks, up_weight, preferred_element_type=jnp.float32
    )
    output_low = (middle + branch_two).astype(jnp.bfloat16)
    grad_middle_norm, grad_gain_two, grad_shift_two = norm_two_back(grad_norm_two)
    grad_middle = cotangent.astype(jnp.float32) + grad_middle_norm
    grad_branch_low = grad_middle.astype(jnp.bfloat16)
    grad_out_bias = jnp.sum(grad_branch_low, axis=0, dtype=jnp.float32)
    grad_out_weight = jnp.dot(attended_low.T, grad_branch_low, preferred_element_type=jnp.float32)
    grad_attended_low = jnp.dot(
        grad_branch_low, attention_weights[3].T, preferred_element_type=jnp.float32
    ).astype(jnp.bfloat16)

    def head_backward(pieces):
        query_head, key_head, value_head, grad_head, log_total = pieces
        scores = head_scores(query_head, key_head)
        probs = jnp.exp(scores - log_total[:, None])
        grad_probs = jnp.dot(grad_head, value_head.T, preferred_element_type=jnp.float32)
        inner = jnp.sum(probs * grad_probs, axis=1, keepdims=True)
        grad_scores = (probs * (grad_probs - inner)).astype(jnp.bfloat16)
        grad_query = (
            jnp.dot(grad_scores, key_head, preferred_element_type=jnp.float32) * score_scale
        )
        grad_key = (
            jnp.dot(grad_scores.T, query_head, preferred_element_type=jnp.float32) * score_scale
        )
        grad_value = jnp.dot(
            probs.astype(jnp.bfloat16).T, grad_head, preferred_element_type=jnp.float32
        )
        return (grad_query, grad_key, grad_value)

    grad_queries, grad_keys, grad_values = lax.map(
        head_backward,
        (query_heads, key_heads, value_heads, heads_first(grad_attended_low), log_totals),
    )
    grad_query_lin, grad_freq_query = query_back(tokens_first(grad_queries))
    grad_key_lin, grad_freq_key = key_back(tokens_first(grad_keys))
    grad_query_low = grad_query_lin.astype(jnp.bfloat16)
    grad_key_low = grad_key_lin.astype(jnp.bfloat16)
    grad_value_low = tokens_first(grad_values).astype(jnp.bfloat16)
    grad_query_weight = jnp.dot(norm_one_low.T, grad_query_low, preferred_element_type=jnp.float32)
    grad_key_weight = jnp.dot(norm_one_low.T, grad_key_low, preferred_element_type=jnp.float32)
    grad_value_weight = jnp.dot(norm_one_low.T, grad_value_low, preferred_element_type=jnp.float32)
    grad_norm_one = jnp.dot(
        grad_query_low, attention_weights[0].T, preferred_element_type=jnp.float32
    )
    grad_norm_one = grad_norm_one + jnp.dot(
        grad_key_low, attention_weights[1].T, preferred_element_type=jnp.float32
    )
    grad_norm_one = grad_norm_one + jnp.dot(
        grad_value_low, attention_weights[2].T, preferred_element_type=jnp.float32
    )
    grad_input_norm, grad_gain_one, grad_shift_one = norm_one_back(grad_norm_one)
    input_grad = grad_middle + grad_input_norm
    head_rows = jnp.stack(
        [
            grad_gain_one,
            grad_shift_one,
            jnp.sum(grad_query_low, axis=0, dtype=jnp.float32),
            jnp.sum(grad_key_low, axis=0, dtype=jnp.float32),
            jnp.sum(grad_value_low, axis=0, dtype=jnp.float32),
            grad_out_bias,
            grad_gain_two,
            grad_shift_two,
        ]
    )
    tail_rows = jnp.stack(
        [jnp.sum(cotangent, axis=0, dtype=jnp.float32), grad_freq_query + grad_freq_key]
    )
    local_vectors = jnp.concatenate([head_rows, up_grad_rows, tail_rows], axis=0)
    vector_sum = lax.psum(local_vectors, ("dp", "mlp"))
    attention_grads = jnp.stack(
        [grad_query_weight, grad_key_weight, grad_value_weight, grad_out_weight]
    )
    attention_share, up_share, down_share = (
        lax.psum_scatter(
            attention_grads.astype(jnp.bfloat16), "mlp", scatter_dimension=0, tiled=True
        ).astype(jnp.float32),
        lax.psum_scatter(
            grad_up.astype(jnp.bfloat16), "mlp", scatter_dimension=0, tiled=True
        ).astype(jnp.float32),
        lax.psum_scatter(
            grad_down.astype(jnp.bfloat16), "mlp", scatter_dimension=0, tiled=True
        ).astype(jnp.float32),
    )
    grad_stack = jnp.concatenate([attention_share, up_share, down_share], axis=0)
    reduced = lax.psum(grad_stack, "dp")
    block_kind = jnp.sum(jnp.where(holds_block, jnp.arange(3, dtype=jnp.int32), 0))
    owns_block = jnp.any(holds_block)
    gradient = jnp.take(reduced, block_kind, axis=0)
    decay_matrix = decays[0]
    left_old = left_slots[0, 0]
    right_old = right_slots[0, 0]
    master_old = master_slots[0, 0]
    left_next = decay_matrix * left_old + (1.0 - decay_matrix) * jnp.dot(
        gradient, gradient.T, precision=lax.Precision.HIGHEST
    )
    right_next = decay_matrix * right_old + (1.0 - decay_matrix) * jnp.dot(
        gradient.T, gradient, precision=lax.Precision.HIGHEST
    )
    direction = jnp.dot(
        jnp.dot(left_roots[0, 0], gradient, precision=lax.Precision.HIGHEST),
        right_roots[0, 0],
        precision=lax.Precision.HIGHEST,
    )
    normed_step = direction * lax.rsqrt(jnp.mean(direction * direction) + GRAFT_EPSILON)
    master_next = master_old - RATE_MATRIX * normed_step
    slot_grad = jnp.where(owns_block, gradient, 0.0)[None, None]
    left_out = jnp.where(owns_block, left_next, left_old)[None, None]
    right_out = jnp.where(owns_block, right_next, right_old)[None, None]
    master_out = jnp.where(owns_block, master_next, master_old)[None, None]
    share_width = model_width // groups_mlp

    def own_columns(table):
        return lax.dynamic_slice_in_dim(table, mlp_index * share_width, share_width, 1)

    grad_share = own_columns(vector_sum)
    moment_old = own_columns(vector_moments)
    vector_old = own_columns(vectors)
    decay_vector = decays[1]
    moment_next = decay_vector * moment_old + (1.0 - decay_vector) * grad_share * grad_share
    vector_next = vector_old - RATE_VECTOR * grad_share / (jnp.sqrt(moment_next) + STEP_EPSILON)
    return (
        output_low,
        input_grad,
        slot_grad,
        left_out,
        right_out,
        master_out,
        grad_share,
        moment_next,
        vector_next,
    )


def solution(mesh):
    placed = (
        P(("dp", "mlp"), None),
        P(("dp", "mlp"), None),
        P(),
        P(),
        P(),
        P(),
        P("dp", "mlp", None, None),
        P("dp", "mlp", None, None),
        P("dp", "mlp", None, None),
        P("dp", "mlp", None, None),
        P("dp", "mlp", None, None),
        P(("dp", "mlp")),
        P(("dp", "mlp")),
        P(("dp", "mlp")),
        P(("dp", "mlp")),
        P(("dp", "mlp")),
    )
    return jax.shard_map(
        local,
        mesh=mesh,
        in_specs=placed,
        out_specs=(
            P(("dp", "mlp"), None),
            P(("dp", "mlp"), None),
            P("dp", "mlp", None, None),
            P("dp", "mlp", None, None),
            P("dp", "mlp", None, None),
            P("dp", "mlp", None, None),
            P(None, "mlp"),
            P(None, "mlp"),
            P(None, "mlp"),
        ),
        check_vma=False,
    )
```

profile of v0, /device:TPU:0, one launch (start us, length us, event | category | flops | bytes accessed | tf_op | source)
XLA Modules:
  0.0 1202.3 jit_solution(14143546167382789815)
XLA Ops:
  8.8 5.2 broadcast_select_fusion
  14.0 278.3 %all-reduce.12 = bf16[3,768,768]{2,1,0:T(8,128)(2,1)} all-reduce(f32[3,768,768]{2,1,0:T(8,128)} %broadcast_select_fusion), channel_id=1, replica_groups=mesh['dp'=8,'mlp'=4] {'dp'}, use_global_device_ids=true, to_apply=%region_2.3 | all-reduce | flops 1769472 | bytes 10616832 | tf_op jit(solution)/shard_map/psum | solution.py:92
  303.2 78.7 %all-gather.3.cloned.1.call-done = bf16[12,768,768]{2,1,0:T(8,128)(2,1)} async-done(((bf16[3,768,768]{2,1,0:T(8,128)(2,1)}), bf16[12,768,768]{2,1,0:T(8,128)(2,1)}) %all-gather.3.cloned.1.call-update) | async-done | bytes 14155792 | tf_op jit(solution)/shard_map/all_gather | solution.py:97
  381.8 4.9 slice_bitcast_fusion.3
  393.6 7.7 subtract_convert_fusion
  409.1 4.1 copy.103
  413.2 4.5 add_convert_fusion.4
  421.8 85.7 %while.32 = (s32[]{:T(128)}, bf16[12,1024,64]{1,2,0:T(8,128)(2,1)}, f32[12,1024]{1,0:T(8,128)}, bf16[12,1024,64]{2,1,0:T(8,128)(2,1)}, bf16[12,1024,64]{2,1,0:T(...) while((s32[]{:T(128)}, bf16[12,1024,64]{1,2,0:T(8,128)(2,1)}, ...), condition=%wide.region_8.9_spmd.clone.clone, body=%wide.region_5.8_spmd.clone.sunk.clone | while | flops 284163072 | bytes 13695065 | solution.py:141
  507.5 10.2 fusion.64
  517.7 12.7 %copy.133 = f32[1024,3072]{1,0:T(8,128)} copy(f32[1024,3072]{0,1:T(8,128)} %bitcast.277) | data formatting | bytes 25165824 | tf_op jit(solution)/shard_map/reshape | solution.py:165
  530.3 6.6 copy.105
  544.0 40.9 %convert_reduce_fusion = (f32[3072]{0:T(1024)}, bf16[1024,3072]{1,0:T(8,128)(2,1)}, f32[1024,3072]{1,0:T(8,128)}, f32[1024,3072]{1,0:T(8,128)}) fusion(f32[1024,3072]{1,0:T(8,128)S(1)} %copy-done.14, f32[3072]{0:T(1024)S(1)} %add.236, bf16[3072,768]{1,0:T(8,128)(2,1)} %bitcast.289, f32[1024,768]{0,1:T(8,128)S(1)} %get-tuple-element.370, ...), kind=kOutput, calls=%fused_computation.58 | convolution fusion | flops 5071696896 | bytes 51943424 | tf_op jit(solution)/shard_map/td,mde->tme/dot_general | solution.py:150
  584.9 12.8 %multiply_convert_fusion.1 = bf16[1024,3072]{1,0:T(8,128)(2,1)} fusion(f32[1024,3072]{1,0:T(8,128)} %get-tuple-element.336, f32[1024,3072]{1,0:T(8,128)} %get-tuple-element.371, f32[3072]{0:T(1024)S(1)} %add.236), kind=kLoop, calls=%fused_computation.60 | loop fusion | flops 12582912 | bytes 31469568 | tf_op jit(solution)/shard_map/convert_element_type | solution.py:156
  597.8 8.6 copy.137
  606.4 9.0 convolution_convert_fusion
  618.0 8.8 copy.138
  626.8 9.9 fusion.141
  647.4 4.4 convolution_convert_fusion.1
  655.9 10.4 convert_bitcast_fusion
  667.0 159.3 %while.33 = (s32[]{:T(128)}, f32[12,1024,64]{1,2,0:T(8,128)}, f32[12,1024,64]{1,2,0:T(8,128)}, bf16[12,1024,64]{1,2,0:T(8,128)(2,1)}, bf16[12,1024,64]{2,1,0:T(8...) while((s32[]{:T(128)}, f32[12,1024,64]{1,2,0:T(8,128)}, ...), condition=%wide.region_15.16_spmd.clone.clone, body=%wide.region_13.15_spmd.clone.sunk.clone | while | flops 681704448 | bytes 34112624 | solution.py:205
  826.3 12.0 multiply_add_fusion.1
  840.7 7.8 multiply_add_fusion
  860.6 48.4 %reduce-scatter.4.cloned.1.call-done = bf16[1,768,768]{2,1,0:T(8,128)(2,1)} async-done(((bf16[4,768,768]{2,1,0:T(8,128)(2,1)}), bf16[1,768,768]{2,1,0:T(8,128)(2,1)}) %reduce-scatter.4.cloned.1.call-update) | async-done | bytes 1179664 | tf_op jit(solution)/shard_map/reduce_scatter | solution.py:249
  909.0 5.3 maximum_convert_fusion
  919.4 10.5 fusion.75
  955.9 45.1 %psum.23 = f32[14,768]{1,0:T(8,128)S(1)} all-reduce(f32[14,768]{1,0:T(8,128)S(1)} %concatenate.21), channel_id=1, replica_groups=mesh['dp'=8,'mlp'=4] {'dp','mlp'}, use_global_device_ids=true, to_apply=%region_39.40 | all-reduce | flops 10752 | bytes 86016 | tf_op jit(solution)/shard_map/psum | solution.py:244
  1003.1 143.9 %all-reduce.11.cloned.1.call-done = f32[3,768,768]{2,1,0:T(8,128)} async-done(((f32[3,768,768]{2,1,0:T(8,128)}), f32[3,768,768]{2,1,0:T(8,128)}) %all-reduce.11.cloned.1.call-update) | async-done | bytes 7077904 | tf_op jit(solution)/shard_map/psum | solution.py:260
  1147.1 13.6 %fusion.79 = f32[768,768]{1,0:T(8,128)S(1)} fusion(f32[1,1,768,768]{3,2,1,0:T(8,128)} %param.29, f32[3,768,768]{2,1,0:T(8,128)} %all-reduce.11.cloned.1.call-done, s32[]{:T(128)S(6)} %select_n.95, pred[]{:T(512)S(6)} %and.13), kind=kOutput, calls=%fused_computation.124 | convolution fusion | flops 5436407808 | bytes 7077893 | tf_op jit(solution)/shard_map/dot_general | solution.py:275
  1160.7 8.7 multiply_reduce_fusion.4
  1170.1 5.0 fusion.76
  1177.5 8.9 fusion.84
  1186.4 9.2 fusion.82
  (347 shorter events, 347.1 us)
Async XLA Ops:
  7.2 1153.5 %copy-start = (f32[1,1,768,768]{3,2,1,0:T(8,128)S(1)}, f32[1,1,768,768]{3,2,1,0:T(8,128)}, u32[]{:S(2)}) copy-start(f32[1,1,768,768]{3,2,1,0:T(8,128)} %param.30) | copy-start | bytes 7077892
  7.2 374.6 %all-gather.3.cloned.1.call-start = ((), (), s32[]{:S(2)}) async-start(), calls=%async_computation.7 | async-start | bytes 17694720 | tf_op jit(solution)/shard_map/all_gather | solution.py:97
  292.3 568.3 %reduce-scatter.8.cloned.1.call-start = ((), (), s32[]{:S(2)}) async-start(), calls=%async_computation.5 | async-start | bytes 5898240 | tf_op jit(solution)/shard_map/reduce_scatter | solution.py:255
  294.8 8.3 copy-start.50
  294.8 8.3 copy-start.51
  297.5 96.0 %copy-start.28 = (f32[12,32]{1,0:T(8,128)}, f32[12,32]{1,0:T(8,128)S(1)}, u32[]{:S(2)}) copy-start(f32[12,32]{1,0:T(8,128)S(1)} %mul.390) | copy-start | bytes 4612
  297.6 95.9 %copy-start.30 = (f32[12,32]{1,0:T(8,128)}, f32[12,32]{1,0:T(8,128)S(1)}, u32[]{:S(2)}) copy-start(f32[12,32]{1,0:T(8,128)S(1)} %mul.385) | copy-start | bytes 4612
  298.4 114.8 %copy-start.40 = (f32[768]{0:T(1024)}, f32[768]{0:T(1024)S(1)}, u32[]{:S(2)}) copy-start(f32[768]{0:T(1024)S(1)} %get-tuple-element.290) | copy-start | bytes 9220
  298.4 114.8 %copy-start.48 = (f32[768]{0:T(1024)}, f32[768]{0:T(1024)S(1)}, u32[]{:S(2)}) copy-start(f32[768]{0:T(1024)S(1)} %get-tuple-element.289) | copy-start | bytes 9220
  300.4 112.8 %copy-start.32 = (f32[1024]{0:T(1024)}, f32[1024]{0:T(1024)S(1)}, u32[]{:S(2)}) copy-start(f32[1024]{0:T(1024)S(1)} %broadcast_multiply_fusion.1) | copy-start | bytes 12292
  302.5 110.7 %copy-start.42 = (f32[1024]{0:T(1024)}, f32[1024]{0:T(1024)S(1)}, u32[]{:S(2)}) copy-start(f32[1024]{0:T(1024)S(1)} %fusion.118) | copy-start | bytes 12292
  303.1 90.4 %copy-start.34 = (f32[1024]{0:T(1024)}, f32[1024]{0:T(1024)S(1)}, u32[]{:S(2)}) copy-start(f32[1024]{0:T(1024)S(1)} %get-tuple-element.377) | copy-start | bytes 12292
  303.1 90.4 %copy-start.36 = (f32[1024]{0:T(1024)}, f32[1024]{0:T(1024)S(1)}, u32[]{:S(2)}) copy-start(f32[1024]{0:T(1024)S(1)} %get-tuple-element.378) | copy-start | bytes 12292
  381.8 4.9 copy-start.1
  393.5 7.8 copy-start.17
  537.0 7.0 copy-start.14
  541.0 43.9 %copy-start.4 = (f32[1024,768]{0,1:T(8,128)}, f32[1024,768]{0,1:T(8,128)S(1)}, u32[]{:S(2)}) copy-start(f32[1024,768]{0,1:T(8,128)S(1)} %get-tuple-element.370) | copy-start | bytes 9437188
  615.4 245.2 %reduce-scatter.6.cloned.1.call-start = ((), (), s32[]{:S(2)}) async-start(), calls=%async_computation.4 | async-start | bytes 5898240 | tf_op jit(solution)/shard_map/reduce_scatter | solution.py:252
  640.2 4.7 copy-start.8
  666.3 242.7 %reduce-scatter.4.cloned.1.call-start = ((), (), s32[]{:S(2)}) async-start(), calls=%async_computation.3 | async-start | bytes 5898240 | tf_op jit(solution)/shard_map/reduce_scatter | solution.py:249
  667.0 159.3 %copy-start.29 = (f32[12,32]{1,0:T(8,128)S(1)}, f32[12,32]{1,0:T(8,128)}, u32[]{:S(2)}) copy-start(f32[12,32]{1,0:T(8,128)} %copy-done.28) | copy-start | bytes 4612
  667.0 159.3 %copy-start.31 = (f32[12,32]{1,0:T(8,128)S(1)}, f32[12,32]{1,0:T(8,128)}, u32[]{:S(2)}) copy-start(f32[12,32]{1,0:T(8,128)} %copy-done.30) | copy-start | bytes 4612
  667.0 159.3 %copy-start.35 = (f32[1024]{0:T(1024)S(1)}, f32[1024]{0:T(1024)}, u32[]{:S(2)}) copy-start(f32[1024]{0:T(1024)} %copy-done.34) | copy-start | bytes 12292
  667.0 159.3 %copy-start.37 = (f32[1024]{0:T(1024)S(1)}, f32[1024]{0:T(1024)}, u32[]{:S(2)}) copy-start(f32[1024]{0:T(1024)} %copy-done.36) | copy-start | bytes 12292
  826.3 12.3 %copy-start.18 = (f32[12,1024,64]{1,2,0:T(8,128)S(1)}, f32[12,1024,64]{1,2,0:T(8,128)}, u32[]{:S(2)}) copy-start(f32[12,1024,64]{1,2,0:T(8,128)} %get-tuple-element.104) | copy-start | bytes 9437188
  838.5 17.7 %copy-start.25 = (bf16[1024,12,64]{0,2,1:T(8,128)(2,1)}, bf16[1024,12,64]{0,2,1:T(8,128)(2,1)S(1)}, u32[]{:S(2)}) copy-start(bf16[1024,12,64]{0,2,1:T(8,128)(2,1)S(1)} %get-tuple-element.342) | copy-start | bytes 4718596
  860.3 286.7 %all-reduce.11.cloned.1.call-start = ((), (), s32[]{:S(2)}) async-start(), calls=%async_computation.6 | async-start | bytes 14155776 | tf_op jit(solution)/shard_map/psum | solution.py:260
  914.4 5.1 copy-start.47
  947.5 5.5 copy-start.46
  951.0 50.0 %copy-start.39 = (f32[14,768]{1,0:T(8,128)S(1)}, f32[14,768]{1,0:T(8,128)}, u32[]{:S(2)}) copy-start(f32[14,768]{1,0:T(8,128)} %param.22) | copy-start | bytes 129028
  1170.1 5.0 copy-start.19
  1177.5 8.9 copy-start.56
  (31 other events, 82.1 us)
Sparse Core Ops, SparseCore 0:
  292.4 89.3 all-gather.2
  615.5 47.9 reduce-scatter.7
  666.4 48.3 reduce-scatter.5
  860.4 48.5 reduce-scatter.3
  914.5 232.5 all-reduce.10
where the time goes:
time: 1220 us; the launch traced here: 1200 us
  matrix products  359 us (29%)
  blocking collectives  323 us (26%)
  waiting for transfers between devices  271 us (22%)
  local copies, waits for them, and re-layouts  115 us (9%)
  other arithmetic  115 us (9%)
  between operations  18.4 us (2%)
    psum x1, blocking collectives, local(): blocks = lax.psum(owned_blocks, 'dp')  278 us
    psum x1, waiting for transfers between devices, local(): reduced = lax.psum(grad_stack, 'dp')  144 us
    all_gather x1, waiting for transfers between devices, local(): every_block = lax.all_gather(blocks_low[None], 'mlp', axis=0, tiled=True)  78.7 us
    dot_general x24, matrix products, head_scores(): jnp.dot(query_head, key_head.T, preferred_element_type=jnp.float32)  52.2 us
    reduce_scatter x1, waiting for transfers between devices, local(): lax.psum_scatter(attention_grads.astype(jnp.bfloat16), 'mlp', scatter_dim...  48.4 us
    psum x1, blocking collectives, local(): vector_sum = lax.psum(local_vectors, ('dp', 'mlp'))  45.1 us
    dot_general x1, matrix products, local(): jnp.einsum('td,mde->tme', norm_two_low, up_weight, preferred_element_type...  40.9 us
    dot_general x12, matrix products, head_forward(): jnp.dot(weights_low, value_head, preferred_element_type=jnp.float32)  35.5 us
  transfers between devices with their start and end apart: 5, of which 3 were waited for; matrix products, arithmetic and copies ran while one was open for 24% of the time, Pallas kernels for 0%

commit v1 on v0

--- a/solution.py
+++ b/solution.py
@@ -94,7 +94,9 @@
     up_rows = vectors[8 : 8 + groups_mlp]
     down_bias = vectors[8 + groups_mlp]
     freq_row = vectors[9 + groups_mlp]
-    every_block = lax.all_gather(blocks_low[None], "mlp", axis=0, tiled=True)
+    every_block = jnp.concatenate(
+        lax.all_to_all(jnp.stack([blocks_low[None]] * lax.axis_size("mlp")), "mlp", 0, 0), axis=0
+    )
     attention_weights = every_block[:, 0]
     up_weight = every_block[:, 1]
     down_weight = every_block[:, 2]

time: 1220 us -> 1300 us (1.066)
  waiting for transfers between devices: 271 us -> 334 us
  local copies, waits for them, and re-layouts: 115 us -> 129 us
    all_to_all x0 -> x1, waiting for transfers between devices: none -> 145 us  [local(): lax.all_to_all(jnp.stack([blocks_low[None]] * lax.axis_size('mlp')), 'mlp...]
    all_gather x1 -> x0, waiting for transfers between devices: 78.7 us -> none  [local(): every_block = lax.all_gather(blocks_low[None], 'mlp', axis=0, tiled=True)]
    unnamed x121 -> x123, local copies, waits for them, and re-layouts: 33.5 us -> 36.1 us
  transfers between devices with their start and end apart: 5 -> 5, of which waited for: 3 -> 3; matrix products, arithmetic and copies ran while one was open for 24% -> 22% of each run, Pallas kernels for 0% -> 0%
where the time goes in v1:
time: 1300 us; the launch traced here: 1280 us
  matrix products  355 us (27%)
  waiting for transfers between devices  334 us (26%)
  blocking collectives  323 us (25%)
  local copies, waits for them, and re-layouts  129 us (10%)
  other arithmetic  114 us (9%)
  between operations  18.4 us (1%)
    psum x1, blocking collectives, local(): blocks = lax.psum(owned_blocks, 'dp')  278 us
    all_to_all x1, waiting for transfers between devices, local(): lax.all_to_all(jnp.stack([blocks_low[None]] * lax.axis_size('mlp')), 'mlp...  145 us
    psum x1, waiting for transfers between devices, local(): reduced = lax.psum(grad_stack, 'dp')  144 us
    dot_general x24, matrix products, head_scores(): jnp.dot(query_head, key_head.T, preferred_element_type=jnp.float32)  52.3 us
    reduce_scatter x1, waiting for transfers between devices, local(): lax.psum_scatter(attention_grads.astype(jnp.bfloat16), 'mlp', scatter_dim...  45.3 us
    psum x1, blocking collectives, local(): vector_sum = lax.psum(local_vectors, ('dp', 'mlp'))  45.2 us
    dot_general x1, matrix products, local(): jnp.einsum('td,mde->tme', norm_two_low, up_weight, preferred_element_type...  40.9 us
    unnamed x123, local copies, waits for them, and re-layouts  36.1 us
  transfers between devices with their start and end apart: 5, of which 3 were waited for; matrix products, arithmetic and copies ran while one was open for 22% of the time, Pallas kernels for 0%

profile of v1, /device:TPU:0, one launch (start us, length us, event | category | flops | bytes accessed | tf_op | source)
XLA Modules:
  0.0 1281.9 jit_solution(8047192213544388597)
XLA Ops:
  8.7 5.2 broadcast_select_fusion
  13.9 278.3 %all-reduce.12 = bf16[3,768,768]{2,1,0:T(8,128)(2,1)} all-reduce(f32[3,768,768]{2,1,0:T(8,128)} %broadcast_select_fusion), channel_id=1, replica_groups=mesh['dp'=8,'mlp'=4] {'dp'}, use_global_device_ids=true, to_apply=%region_2.3 | all-reduce | flops 1769472 | bytes 10616832 | tf_op jit(solution)/shard_map/psum | solution.py:92
  292.2 6.4 stack.45
  298.6 6.5 all-to-all-start
  315.4 144.6 %all-to-all-done = bf16[4,1,3,768,768]{4,3,2,1,0:T(8,128)(2,1)} async-done(((bf16[4,1,3,768,768]{4,3,2,1,0:T(8,128)(2,1)}), bf16[4,1,3,768,768]{4,3,2,1,0:T(8,128)(2,1)}, u32[]{:S(2)}, u32[]{:S(2)}) %all-to-all-start) | async-done | bytes 14155808 | tf_op jit(solution)/shard_map/all_to_all | solution.py:98
  460.1 7.4 copy.134
  475.9 7.7 subtract_convert_fusion
  495.5 4.5 add_convert_fusion.4
  504.1 85.7 %while.32 = (s32[]{:T(128)}, bf16[12,1024,64]{1,2,0:T(8,128)(2,1)}, f32[12,1024]{1,0:T(8,128)}, bf16[12,1024,64]{2,1,0:T(8,128)(2,1)}, bf16[12,1024,64]{2,1,0:T(...) while((s32[]{:T(128)}, bf16[12,1024,64]{1,2,0:T(8,128)(2,1)}, ...), condition=%wide.region_8.9_spmd.clone.clone, body=%wide.region_5.8_spmd.clone.sunk.clone | while | flops 284163072 | bytes 13695065 | solution.py:143
  589.8 10.2 fusion.64
  600.0 12.7 copy.129
  612.7 6.6 copy.102
  626.3 40.9 %convert_reduce_fusion = (f32[3072]{0:T(1024)}, bf16[1024,3072]{1,0:T(8,128)(2,1)}, f32[1024,3072]{1,0:T(8,128)}, f32[1024,3072]{1,0:T(8,128)}) fusion(f32[1024,3072]{1,0:T(8,128)S(1)} %copy-done.15, f32[3072]{0:T(1024)S(1)} %add.236, bf16[3072,768]{1,0:T(8,128)(2,1)} %bitcast.298, f32[1024,768]{0,1:T(8,128)S(1)} %get-tuple-element.370, ...), kind=kOutput, calls=%fused_computation.59 | convolution fusion | flops 5071696896 | bytes 51943424 | tf_op jit(solution)/shard_map/td,mde->tme/dot_general | solution.py:152
  667.3 12.8 %multiply_convert_fusion.1 = bf16[1024,3072]{1,0:T(8,128)(2,1)} fusion(f32[1024,3072]{1,0:T(8,128)} %get-tuple-element.336, f32[1024,3072]{1,0:T(8,128)} %get-tuple-element.371, f32[3072]{0:T(1024)S(1)} %add.236), kind=kLoop, calls=%fused_computation.61 | loop fusion | flops 12582912 | bytes 31469568 | tf_op jit(solution)/shard_map/convert_element_type | solution.py:158
  680.1 8.6 copy.131
  688.7 9.0 convolution_convert_fusion
  700.4 9.0 copy.132
  709.4 9.8 fusion.141
  738.5 10.3 convert_bitcast_fusion
  749.5 159.3 %while.33 = (s32[]{:T(128)}, f32[12,1024,64]{1,2,0:T(8,128)}, f32[12,1024,64]{1,2,0:T(8,128)}, bf16[12,1024,64]{1,2,0:T(8,128)(2,1)}, bf16[12,1024,64]{2,1,0:T(8...) while((s32[]{:T(128)}, f32[12,1024,64]{1,2,0:T(8,128)}, ...), condition=%wide.region_15.16_spmd.clone.clone, body=%wide.region_13.15_spmd.clone.sunk.clone | while | flops 681704448 | bytes 34112624 | solution.py:207
  908.9 12.0 multiply_add_fusion.1
  923.3 7.8 multiply_add_fusion
  943.2 45.3 %reduce-scatter.4.cloned.1.call-done = bf16[1,768,768]{2,1,0:T(8,128)(2,1)} async-done(((bf16[4,768,768]{2,1,0:T(8,128)(2,1)}), bf16[1,768,768]{2,1,0:T(8,128)(2,1)}) %reduce-scatter.4.cloned.1.call-update) | async-done | bytes 1179664 | tf_op jit(solution)/shard_map/reduce_scatter | solution.py:251
  988.6 5.3 maximum_convert_fusion
  999.0 10.5 fusion.75
  1035.4 45.2 %psum.23 = f32[14,768]{1,0:T(8,128)S(1)} all-reduce(f32[14,768]{1,0:T(8,128)S(1)} %concatenate.21), channel_id=1, replica_groups=mesh['dp'=8,'mlp'=4] {'dp','mlp'}, use_global_device_ids=true, to_apply=%region_39.40 | all-reduce | flops 10752 | bytes 86016 | tf_op jit(solution)/shard_map/psum | solution.py:246
  1082.7 143.9 %all-reduce.11.cloned.1.call-done = f32[3,768,768]{2,1,0:T(8,128)} async-done(((f32[3,768,768]{2,1,0:T(8,128)}), f32[3,768,768]{2,1,0:T(8,128)}) %all-reduce.11.cloned.1.call-update) | async-done | bytes 7077904 | tf_op jit(solution)/shard_map/psum | solution.py:262
  1226.6 13.6 %fusion.79 = f32[768,768]{1,0:T(8,128)S(1)} fusion(f32[1,1,768,768]{3,2,1,0:T(8,128)} %param.29, f32[3,768,768]{2,1,0:T(8,128)} %all-reduce.11.cloned.1.call-done, s32[]{:T(128)S(6)} %select_n.95, pred[]{:T(512)S(6)} %and.13), kind=kOutput, calls=%fused_computation.125 | convolution fusion | flops 5436407808 | bytes 7077893 | tf_op jit(solution)/shard_map/dot_general | solution.py:277
  1240.2 8.7 multiply_reduce_fusion.4
  1249.7 5.0 fusion.76
  1257.1 8.9 fusion.84
  1265.9 9.2 fusion.82
  (350 shorter events, 356.8 us)
Async XLA Ops:
  7.2 1233.0 %copy-start = (f32[1,1,768,768]{3,2,1,0:T(8,128)S(1)}, f32[1,1,768,768]{3,2,1,0:T(8,128)}, u32[]{:S(2)}) copy-start(f32[1,1,768,768]{3,2,1,0:T(8,128)} %param.30) | copy-start | bytes 7077892
  298.6 161.5 %all-to-all-start = ((bf16[4,1,3,768,768]{4,3,2,1,0:T(8,128)(2,1)}), bf16[4,1,3,768,768]{4,3,2,1,0:T(8,128)(2,1)}, u32[]{:S(2)}, u32[]{:S(2)}) async-start(bf16[4,1,3,768,768]{4,3,2,1,0:T(8,128)(2,1)} %stack.45), calls=%async_computation | async-start | bytes 28311552 | tf_op jit(solution)/shard_map/all_to_all | solution.py:98
  305.1 638.1 %reduce-scatter.8.cloned.1.call-start = ((), (), s32[]{:S(2)}) async-start(), calls=%async_computation.6 | async-start | bytes 5898240 | tf_op jit(solution)/shard_map/reduce_scatter | solution.py:257
  307.7 7.7 copy-start.51
  307.7 7.7 copy-start.52
  310.4 165.4 %copy-start.29 = (f32[12,32]{1,0:T(8,128)}, f32[12,32]{1,0:T(8,128)S(1)}, u32[]{:S(2)}) copy-start(f32[12,32]{1,0:T(8,128)S(1)} %mul.390) | copy-start | bytes 4612
  310.5 165.4 %copy-start.31 = (f32[12,32]{1,0:T(8,128)}, f32[12,32]{1,0:T(8,128)S(1)}, u32[]{:S(2)}) copy-start(f32[12,32]{1,0:T(8,128)S(1)} %mul.385) | copy-start | bytes 4612
  311.2 184.3 %copy-start.41 = (f32[768]{0:T(1024)}, f32[768]{0:T(1024)S(1)}, u32[]{:S(2)}) copy-start(f32[768]{0:T(1024)S(1)} %get-tuple-element.290) | copy-start | bytes 9220
  311.2 184.3 %copy-start.49 = (f32[768]{0:T(1024)}, f32[768]{0:T(1024)S(1)}, u32[]{:S(2)}) copy-start(f32[768]{0:T(1024)S(1)} %get-tuple-element.289) | copy-start | bytes 9220
  312.9 182.6 %copy-start.33 = (f32[1024]{0:T(1024)}, f32[1024]{0:T(1024)S(1)}, u32[]{:S(2)}) copy-start(f32[1024]{0:T(1024)S(1)} %broadcast_multiply_fusion.1) | copy-start | bytes 12292
  314.8 180.7 %copy-start.43 = (f32[1024]{0:T(1024)}, f32[1024]{0:T(1024)S(1)}, u32[]{:S(2)}) copy-start(f32[1024]{0:T(1024)S(1)} %fusion.118) | copy-start | bytes 12292
  315.4 160.4 %copy-start.35 = (f32[1024]{0:T(1024)}, f32[1024]{0:T(1024)S(1)}, u32[]{:S(2)}) copy-start(f32[1024]{0:T(1024)S(1)} %get-tuple-element.377) | copy-start | bytes 12292
  315.4 160.4 %copy-start.37 = (f32[1024]{0:T(1024)}, f32[1024]{0:T(1024)S(1)}, u32[]{:S(2)}) copy-start(f32[1024]{0:T(1024)S(1)} %get-tuple-element.378) | copy-start | bytes 12292
  467.5 6.7 copy-start.4
  475.8 7.8 copy-start.18
  619.3 7.0 copy-start.15
  623.3 43.9 %copy-start.5 = (f32[1024,768]{0,1:T(8,128)}, f32[1024,768]{0,1:T(8,128)S(1)}, u32[]{:S(2)}) copy-start(f32[1024,768]{0,1:T(8,128)S(1)} %get-tuple-element.370) | copy-start | bytes 9437188
  697.7 245.5 %reduce-scatter.6.cloned.1.call-start = ((), (), s32[]{:S(2)}) async-start(), calls=%async_computation.5 | async-start | bytes 5898240 | tf_op jit(solution)/shard_map/reduce_scatter | solution.py:254
  722.7 4.8 copy-start.9
  748.8 239.7 %reduce-scatter.4.cloned.1.call-start = ((), (), s32[]{:S(2)}) async-start(), calls=%async_computation.4 | async-start | bytes 5898240 | tf_op jit(solution)/shard_map/reduce_scatter | solution.py:251
  749.5 159.4 %copy-start.30 = (f32[12,32]{1,0:T(8,128)S(1)}, f32[12,32]{1,0:T(8,128)}, u32[]{:S(2)}) copy-start(f32[12,32]{1,0:T(8,128)} %copy-done.29) | copy-start | bytes 4612
  749.5 159.4 %copy-start.32 = (f32[12,32]{1,0:T(8,128)S(1)}, f32[12,32]{1,0:T(8,128)}, u32[]{:S(2)}) copy-start(f32[12,32]{1,0:T(8,128)} %copy-done.31) | copy-start | bytes 4612
  749.5 159.4 %copy-start.36 = (f32[1024]{0:T(1024)S(1)}, f32[1024]{0:T(1024)}, u32[]{:S(2)}) copy-start(f32[1024]{0:T(1024)} %copy-done.35) | copy-start | bytes 12292
  749.5 159.4 %copy-start.38 = (f32[1024]{0:T(1024)S(1)}, f32[1024]{0:T(1024)}, u32[]{:S(2)}) copy-start(f32[1024]{0:T(1024)} %copy-done.37) | copy-start | bytes 12292
  908.9 12.3 copy-start.19
  921.1 17.7 %copy-start.26 = (bf16[1024,12,64]{0,2,1:T(8,128)(2,1)}, bf16[1024,12,64]{0,2,1:T(8,128)(2,1)S(1)}, u32[]{:S(2)}) copy-start(bf16[1024,12,64]{0,2,1:T(8,128)(2,1)S(1)} %get-tuple-element.342) | copy-start | bytes 4718596
  942.9 283.7 %all-reduce.11.cloned.1.call-start = ((), (), s32[]{:S(2)}) async-start(), calls=%async_computation.7 | async-start | bytes 14155776 | tf_op jit(solution)/shard_map/psum | solution.py:262
  993.9 5.1 copy-start.48
  1027.0 5.5 copy-start.47
  1030.6 50.0 %copy-start.40 = (f32[14,768]{1,0:T(8,128)S(1)}, f32[14,768]{1,0:T(8,128)}, u32[]{:S(2)}) copy-start(f32[14,768]{1,0:T(8,128)} %param.22) | copy-start | bytes 129028
  1249.7 5.0 copy-start.20
  1257.1 8.9 copy-start.57
  (32 other events, 85.1 us)
Sparse Core Ops, SparseCore 0:
  697.9 45.3 reduce-scatter.7
  749.0 45.4 reduce-scatter.5
  943.0 45.4 reduce-scatter.3
  994.1 232.5 all-reduce.10
